TPU v7x, 256 devices: a whole 4x4x8 slice. The times are simulated.
256 devices in a mesh: context: 16 (over z, core), heads: 16 (over x, y).
Axes of the slice: x: 4, y: 4, z: 8, core: 2. Of those that a mesh axis runs over, the one named last changes fastest.
Arguments:
- main_query: bfloat16 [256, 128, 576], P('context', 'heads'), may hold values from -6 to 6
- latent_keys: bfloat16 [32768, 576], P('context'), may hold values from -6 to 6
- head_lse: float32 [256, 128], P(None, 'heads'), may hold values from 4 to 8
- lengths: int32 [256], replicated, may hold values from 1 to 32768, as said below
- index_query: bfloat16 [256, 64, 128], P('heads'), may hold values from -256 to 256
- index_key: bfloat16 [32768, 128], P('context'), may hold values from -8 to 8
- index_weight: float32 [256, 64], P('heads'), may hold values from -2.4 to 2.4
Outputs:
- grad_index_query: float32 [256, 64, 128], P('heads', 'context')
- grad_index_key: float32 [32768, 128], P(('context', 'heads'))
Inputs may be any that keep to these rules, and one draw needn't show every extreme that they name: Query rows come in blocks of 16 consecutive rows whose lengths rise by one from row to row; some block ends at the last key.
All inputs are finite; a program needn't handle non-finite values.
Results may differ from a plain program's by a relative error of at most 0.0029.
Values may be sent and summed in bfloat16 or wider, within the bound.
A program may use at most 64 MiB of HBM per device.

v0:
```python
import math

import jax
import jax.numpy as jnp
from jax import lax
from jax.sharding import PartitionSpec as P

main_scale = 192.0 ** (-0.5)
loss_scale = 64.0
masked_low = -1e30


def head_mass(queries, lse_rows, len_rows, latent, first_key):
    row_count = queries.shape[0]
    block_rows = math.gcd(row_count, 64)
    steps_count = row_count // block_rows
    key_pos = first_key + jnp.arange(latent.shape[0], dtype=jnp.int32)

    def one_block(inputs):
        query_block, lse_block, len_block = inputs
        scores = (
            jnp.einsum("rhd,sd->rhs", query_block, latent, preferred_element_type=jnp.float32)
            * main_scale
        )
        summed = jnp.sum(jnp.exp(scores - lse_block[:, :, None]), axis=1)
        return jnp.where(key_pos[None, :] < len_block[:, None], summed, 0.0)

    stacked = lax.map(
        one_block,
        (
            queries.reshape((steps_count, block_rows) + queries.shape[1:]),
            lse_rows.reshape(steps_count, block_rows, lse_rows.shape[1]),
            len_rows.reshape(steps_count, block_rows),
        ),
    )
    return stacked.reshape(row_count, latent.shape[0])


def on_device(main_query, latent_keys, head_lse, lengths, index_query, index_key, index_weight):
    key_count = latent_keys.shape[0]
    first_key = lax.axis_index("context") * key_count
    own_rows = index_query.shape[0]
    row_first = lax.axis_index("heads") * own_rows
    partial_mass = head_mass(
        lax.all_gather(main_query, "context", axis=0, tiled=True),
        head_lse,
        lengths,
        latent_keys,
        first_key,
    )
    summed_mass = lax.psum(partial_mass, "heads")
    row_mass = lax.dynamic_slice_in_dim(summed_mass, row_first, own_rows, 0)
    own_len = lax.dynamic_slice_in_dim(lengths, row_first, own_rows, 0)
    visible = (first_key + jnp.arange(key_count, dtype=jnp.int32))[None, :] < own_len[:, None]
    heads_count = index_query.shape[1]
    width = index_query.shape[2]
    index_scale = width ** (-0.5)
    flat_query = index_query.reshape(own_rows * heads_count, width)
    block_keys = math.gcd(key_count, 512)
    block_total = key_count // block_keys
    key_blocks = index_key.reshape(block_total, block_keys, width)

    def block_dots(key_block):
        products = lax.dot_general(
            flat_query, key_block, (((1,), (1,)), ((), ())), preferred_element_type=jnp.float32
        )
        return products.reshape(own_rows, heads_count, key_block.shape[0])

    def block_logits(key_block):
        return (
            jnp.einsum(
                "tj,tjs->ts",
                index_weight,
                jax.nn.relu(block_dots(key_block)),
                precision=lax.Precision.HIGHEST,
            )
            * index_scale
        )

    logits = jnp.moveaxis(lax.map(block_logits, key_blocks), 0, 1).reshape(own_rows, key_count)
    local_top = jnp.max(jnp.where(visible, logits, masked_low), axis=1)
    mass_local = jnp.sum(row_mass, axis=1)
    top = lax.pmax(local_top, "context")
    weights_exp = jnp.where(visible, jnp.exp(logits - top[:, None]), 0.0)
    share_sum, mass_total = lax.psum((jnp.sum(weights_exp, axis=1), mass_local), "context")
    probability = weights_exp / share_sum[:, None]
    target = row_mass / mass_total[:, None]
    slopes = loss_scale * (probability - target)
    slope_blocks = slopes.reshape(own_rows, block_total, block_keys).transpose(1, 0, 2)

    def back_step(query_grad, inputs):
        key_block, slope_block = inputs
        products = block_dots(key_block)
        terms = jnp.where(
            products > 0, slope_block[:, None, :] * index_weight[:, :, None] * index_scale, 0.0
        )
        terms = terms.astype(jnp.bfloat16).reshape(own_rows * heads_count, key_block.shape[0])
        query_grad = query_grad + jnp.dot(terms, key_block, preferred_element_type=jnp.float32)
        key_grad = lax.dot_general(
            terms, flat_query, (((0,), (0,)), ((), ())), preferred_element_type=jnp.float32
        )
        return (query_grad, key_grad)

    start_grad = jnp.zeros((own_rows * heads_count, width), jnp.float32)
    query_grad, key_grads = lax.scan(back_step, start_grad, (key_blocks, slope_blocks))
    query_grad = query_grad.reshape(own_rows, heads_count, width)
    key_grad = key_grads.reshape(key_count, width)
    out_query = lax.psum_scatter(query_grad, "context", scatter_dimension=1, tiled=True)
    out_key = lax.psum_scatter(key_grad, "heads", scatter_dimension=0, tiled=True)
    return (out_query, out_key)


def solution(mesh):
    placed = (
        P("context", "heads", None),
        P("context", None),
        P(None, "heads"),
        P(),
        P("heads", None, None),
        P("context", None),
        P("heads", None),
    )
    return jax.shard_map(
        on_device,
        mesh=mesh,
        in_specs=placed,
        out_specs=(P("heads", "context", None), P(("context", "heads"), None)),
        check_vma=False,
    )
```

profile of v0, /device:TPU:1, one launch (start us, length us, event | category | flops | bytes accessed | tf_op | source)
XLA Modules:
  0.0 374.4 jit_solution(15053279912884742428)
XLA Ops:
  7.2 0.7 all-gather.2.cloned.1.call-update
  8.0 0.8 reshape.139
  8.8 0.8 dynamic_slice.31
  9.5 0.8 copy.25
  10.3 0.8 mul.63
  11.1 43.0 %all-gather.2.cloned.1.call-done = bf16[256,8,576]{2,1,0:T(8,128)(2,1)} async-done(((bf16[16,8,576]{2,1,0:T(8,128)(2,1)}), bf16[256,8,576]{2,1,0:T(8,128)(2,1)}) %all-gather.2.cloned.1.call-update) | async-done | bytes 2359312 | tf_op jit(solution)/shard_map/all_gather | solution.py:45
  54.1 22.9 %while.36 = (s32[]{:T(128)}, f32[4,64,2048]{2,1,0:T(8,128)}, s32[4,64]{1,0:T(4,128)S(1)}, bf16[4,64,8,576]{3,2,1,0:T(8,128)(2,1)}, bf16[2048,576]{0,1:T(8,128)(2...) while((s32[]{:T(128)}, f32[4,64,2048]{2,1,0:T(8,128)}, s32[4,64]{1,0:T(4,128)S(1)}, ...), condition=%wide.region_8.9_spmd.clone, body=%wide.region_6.8_spmd.clone.sunk | while | flops 1211238400 | bytes 4611937 | solution.py:28
  54.1 4.8 %exponential_reduce_fusion.2 = f32[64,2048]{1,0:T(8,128)S(1)} fusion(bf16[2048,576]{0,1:T(8,128)(2,1)} %get-tuple-element.382, f32[64,8]{1,0:T(8,128)S(1)} %dynamic-slice_bitcast_fusion.5, bf16[4,64,8,576]{3,2,1,0:T(8,128)(2,1)} %get-tuple-element.381, s32[]{:T(128)} %get-tuple-element.370), kind=kOutput, calls=%fused_computation.7.clone.1 | convolution fusion | flops 1210974208 | bytes 3541504 | tf_op jit(solution)/shard_map/while/body/eval_jaxpr/rhd,sd->rhs/dot_general | solution.py:22
  58.9 0.9 fusion.60
  59.8 4.8 %exponential_reduce_fusion.2 = f32[64,2048]{1,0:T(8,128)S(1)} fusion(bf16[2048,576]{0,1:T(8,128)(2,1)} %get-tuple-element.382, f32[64,8]{1,0:T(8,128)S(1)} %dynamic-slice_bitcast_fusion.5, bf16[4,64,8,576]{3,2,1,0:T(8,128)(2,1)} %get-tuple-element.381, s32[]{:T(128)} %get-tuple-element.370), kind=kOutput, calls=%fused_computation.7.clone.1 | convolution fusion | flops 1210974208 | bytes 3541504 | tf_op jit(solution)/shard_map/while/body/eval_jaxpr/rhd,sd->rhs/dot_general | solution.py:22
  64.6 0.9 fusion.60
  65.6 4.8 %exponential_reduce_fusion.2 = f32[64,2048]{1,0:T(8,128)S(1)} fusion(bf16[2048,576]{0,1:T(8,128)(2,1)} %get-tuple-element.382, f32[64,8]{1,0:T(8,128)S(1)} %dynamic-slice_bitcast_fusion.5, bf16[4,64,8,576]{3,2,1,0:T(8,128)(2,1)} %get-tuple-element.381, s32[]{:T(128)} %get-tuple-element.370), kind=kOutput, calls=%fused_computation.7.clone.1 | convolution fusion | flops 1210974208 | bytes 3541504 | tf_op jit(solution)/shard_map/while/body/eval_jaxpr/rhd,sd->rhs/dot_general | solution.py:22
  70.4 0.9 fusion.60
  71.3 4.8 %exponential_reduce_fusion.2 = f32[64,2048]{1,0:T(8,128)S(1)} fusion(bf16[2048,576]{0,1:T(8,128)(2,1)} %get-tuple-element.382, f32[64,8]{1,0:T(8,128)S(1)} %dynamic-slice_bitcast_fusion.5, bf16[4,64,8,576]{3,2,1,0:T(8,128)(2,1)} %get-tuple-element.381, s32[]{:T(128)} %get-tuple-element.370), kind=kOutput, calls=%fused_computation.7.clone.1 | convolution fusion | flops 1210974208 | bytes 3541504 | tf_op jit(solution)/shard_map/while/body/eval_jaxpr/rhd,sd->rhs/dot_general | solution.py:22
  76.1 0.9 fusion.60
  77.1 0.9 copy-done
  78.1 20.0 %while.35 = (s32[]{:T(128)}, f32[4,16,512]{2,1,0:T(8,128)S(1)}, bf16[4,512,128]{2,1,0:T(8,128)(2,1)S(1)}, bf16[1024,128]{1,0:T(8,128)(2,1)S(1)}, f32[16,64]{1,0:T(8,128)S(1)}, /*index=5*/s32[]{:T(128)}) while((s32[]{:T(128)}, f32[4,16,512]{2,1,0:T(8,128)S(1)}, bf16[4,512,128]{2,1,0:T(8,128)(2,1)S(1)}, bf16[1024,128]{1,0:T(8,128)(2,1)S(1)}, ...), condition=%wide.region_1.2_spmd, body=%wide.region_0.1_spmd.sunk | while | flops 141041664 | bytes 8884301 | solution.py:80
  78.1 1.8 maximum_bitcast_fusion.2
  79.9 1.9 copy.41
  81.8 1.2 fusion.56
  83.1 1.8 maximum_bitcast_fusion.2
  84.9 2.0 copy.41
  86.9 1.2 fusion.56
  88.1 1.8 maximum_bitcast_fusion.2
  89.9 1.9 copy.41
  91.9 1.2 fusion.56
  93.1 1.8 maximum_bitcast_fusion.2
  94.9 1.9 copy.41
  96.9 1.2 fusion.56
  98.3 23.3 %pmax.7 = f32[16]{0:T(128)S(1)} all-reduce(f32[16]{0:T(128)S(1)} %fusion.18), channel_id=1, replica_groups=mesh['context'=16,'heads'=16] {'context'}, use_global_device_ids=true, to_apply=%region_3.4 | all-reduce | flops 16 | bytes 128 | tf_op jit(solution)/shard_map/pmax | solution.py:83
  121.8 53.3 %all-reduce.3.cloned.1.call-done = f32[256,2048]{1,0:T(8,128)} async-done(((f32[256,2048]{1,0:T(8,128)}), f32[256,2048]{1,0:T(8,128)}) %all-reduce.3.cloned.1.call-update) | async-done | bytes 2097168 | tf_op jit(solution)/shard_map/psum | solution.py:51
  175.1 1.0 dynamic-slice_reduce_fusion
  176.2 25.4 %all-reduce = (f32[16]{0:T(128)S(1)}, f32[16]{0:T(128)S(1)}) all-reduce(f32[16]{0:T(128)S(1)} %dynamic-slice_reduce_fusion, f32[16]{0:T(128)S(1)} %fusion.19), channel_id=1, replica_groups=mesh['context'=16,'heads'=16] {'context'}, use_global_device_ids=true, to_apply=%region_11.12 | all-reduce | flops 32 | bytes 256 | tf_op jit(solution)/shard_map/psum | solution.py:85
  201.6 1.0 subtract_multiply_fusion
  202.6 0.7 copy.35
  203.2 26.9 %while.37 = (s32[]{:T(128)}, f32[1024,128]{1,0:T(8,128)S(1)}, f32[4,512,128]{2,1,0:T(8,128)}, bf16[4,512,128]{2,1,0:T(8,128)(2,1)S(1)}, bf16[1024,128]{1,0:T(8,1...) while((s32[]{:T(128)}, f32[1024,128]{1,0:T(8,128)S(1)}, ...), condition=%wide.wide.region_13.14_spmd.clone, body=%wide.wide.region_12.13_spmd.clone.sunk | while | flops 405536768 | bytes 13734523 | solution.py:105
  203.2 0.8 dynamic-slice_bitcast_fusion.6
  204.0 0.2 mul.80
  204.2 1.8 copy.42
  206.1 2.1 select_convert_fusion.3
  208.2 0.6 convolution_add_fusion.3
  208.8 1.1 fusion.67
  210.0 0.8 dynamic-slice_bitcast_fusion.6
  210.7 0.2 mul.80
  211.0 1.8 copy.42
  212.8 2.1 select_convert_fusion.3
  214.9 0.6 convolution_add_fusion.3
  215.5 1.1 fusion.67
  216.7 0.8 dynamic-slice_bitcast_fusion.6
  217.4 0.2 mul.80
  217.7 1.8 copy.42
  219.5 2.1 select_convert_fusion.3
  221.6 0.6 convolution_add_fusion.3
  222.3 1.1 fusion.67
  223.4 0.8 dynamic-slice_bitcast_fusion.6
  224.4 1.8 copy.42
  226.3 2.1 select_convert_fusion.3
  228.4 0.6 convolution_add_fusion.3
  229.0 1.2 fusion.67
  230.2 1.1 copy.27
  231.4 0.5 reduce-scatter.5.cloned.1.call-update
  231.9 53.3 %reduce-scatter.3.cloned.1.call-done = f32[16,4,128]{2,0,1:T(8,128)} async-done(((f32[16,64,128]{2,0,1:T(8,128)}), f32[16,4,128]{2,0,1:T(8,128)}) %reduce-scatter.3.cloned.1.call-update) | async-done | bytes 32784 | tf_op jit(solution)/shard_map/reduce_scatter | solution.py:108
  285.2 1.4 copy.28
  286.5 81.3 %reduce-scatter.5.cloned.1.call-done = f32[128,128]{1,0:T(8,128)} async-done(((f32[2048,128]{1,0:T(8,128)}), f32[128,128]{1,0:T(8,128)}) %reduce-scatter.5.cloned.1.call-update) | async-done | bytes 65552 | tf_op jit(solution)/shard_map/reduce_scatter | solution.py:109
  (37 shorter events, 1.2 us)
Async XLA Ops:
  7.2 46.9 %all-gather.2.cloned.1.call-start = ((), (), s32[]{:S(2)}) async-start(), calls=%async_computation.2 | async-start | bytes 2785280 | tf_op jit(solution)/shard_map/all_gather | solution.py:45
  7.9 167.2 %all-reduce.3.cloned.1.call-start = ((), (), s32[]{:S(2)}) async-start(), calls=%async_computation.3 | async-start | bytes 4194304 | tf_op jit(solution)/shard_map/psum | solution.py:51
  77.0 0.9 copy-start
  77.0 1.1 copy-start.1
  77.0 1.1 copy-start.2
  77.0 208.1 %reduce-scatter.3.cloned.1.call-start = ((), (), s32[]{:S(2)}) async-start(), calls=%async_computation.4 | async-start | bytes 557056 | tf_op jit(solution)/shard_map/reduce_scatter | solution.py:108
  231.3 136.6 %reduce-scatter.5.cloned.1.call-start = ((), (), s32[]{:S(2)}) async-start(), calls=%async_computation.5 | async-start | bytes 1114112 | tf_op jit(solution)/shard_map/reduce_scatter | solution.py:109
Sparse Core Ops, SparseCore 0:
  9.8 44.2 all-gather.1
  77.1 97.9 all-reduce.2
  231.4 53.6 reduce-scatter.2
  289.1 78.7 reduce-scatter.4
where the time goes:
time: 376 us; the launch traced here: 374 us
  waiting for transfers between devices  232 us (62%)
  blocking collectives  48.6 us (13%)
  matrix products  46.5 us (12%)
  local copies, waits for them, and re-layouts  26.6 us (7%)
  between operations  13.8 us (4%)
  other arithmetic  6.2 us (2%)
    reduce_scatter x1, waiting for transfers between devices, on_device(): lax.psum_scatter(key_grad, 'heads', scatter_dimension=0, tiled=True)  81.3 us
    psum x1, waiting for transfers between devices, on_device(): summed_mass = lax.psum(partial_mass, 'heads')  53.3 us
    reduce_scatter x1, waiting for transfers between devices, on_device(): lax.psum_scatter(query_grad, 'context', scatter_dimension=1, tiled=True)  53.3 us
    all_gather x1, waiting for transfers between devices, on_device(): lax.all_gather(main_query, 'context', axis=0, tiled=True)  43 us
    psum x1, blocking collectives, on_device(): lax.psum((jnp.sum(weights_exp, axis=1), mass_local), 'context')  25.4 us
    pmax x1, blocking collectives, on_device(): top = lax.pmax(local_top, 'context')  23.3 us
    dot_general x4, matrix products, one_block(): jnp.einsum('rhd,sd->rhs', query_block, latent, preferred_element_type=jnp...  19.1 us
    dot_general x8, matrix products, block_dots(): lax.dot_general(flat_query, key_block, (((1,), (1,)), ((), ())), preferre...  15.5 us
  transfers between devices with their start and end apart: 4, of which 4 were waited for; matrix products, arithmetic and copies ran while one was open for 7% of the time, Pallas kernels for 0%

commit v1 on v0

v1 whole, which is shorter than its diff:
```python
import functools

import jax
import jax.numpy as jnp
from jax import lax
from jax.experimental import pallas as pl
from jax.experimental.pallas import tpu as pltpu
from jax.sharding import PartitionSpec as P

MESH = pl.DeviceIdType.MESH
F32 = jnp.float32
BF16 = jnp.bfloat16

log2e = 1.4426950408889634
main_scale = 192.0 ** (-0.5)
loss_scale = 64.0
masked_low = -1e30

NC = 16
NH = 16
NZ = 8
ROWS = 16
HL = 8
LAT = 576
WIDE = 512
REST = LAT - WIDE
IDXH = 64
DIM = 128
KEYS = 2048
TILE = 256
BIG = 512
HEADS = 128


def slot_l(i):
    return 14 if i == 4 else 2 + (i - 1) * 4


def slot_r(i):
    return 3 + (i - 1) * 4


def kernel(
    mq_hbm, lat_hbm, lse_hbm, len_ref, iq_hbm, ik_hbm, iw_hbm, oq_ref, ok_ref,
    rx, qpack, qext, lse_all, lseb, kt, iqraw, qf, qjm, qt, iw_all, wb, ik, ikt, logits, mass,
    st_send, st_recv, terms, gk_send, gk_recv, gk_own, gq_send, gq_recv, gq_own, fin_send, fin_recv,
    load_sem, q_ssem, q_rsem, l_ssem, l_rsem, i_ssem, i_rsem, w_ssem, w_rsem,
    zl_send, zl_recv, zs_send, zs_recv, sib_send, sib_recv, st_ssem, st_rsem,
    gk_ssem, gk_rsem, gq_ssem, gq_rsem, fin_ssem, fin_rsem,
):
    me_c = lax.axis_index("context")
    me_h = lax.axis_index("heads")
    z = me_c // 2
    core = lax.rem(me_c, 2)
    way = 1 - 2 * core
    sibling = me_c + way

    def ctx_of(step, parity):
        return 2 * lax.rem(z + step + 2 * NZ, NZ) + parity

    next_c = ctx_of(way, core)
    prev_c = ctx_of(-way, core)

    source = {0: me_c, 1: sibling}
    for i in range(1, 5):
        source[slot_l(i)] = ctx_of(-way * i, core)
        source[slot_l(i) + (1 if i == 4 else 2)] = ctx_of(way * i, 1 - core)
    for i in range(1, 4):
        source[slot_r(i)] = ctx_of(way * i, core)
        source[slot_r(i) + 2] = ctx_of(-way * i, 1 - core)

    def plane(o):
        return lax.rem(me_h + o, NH)

    def line(o):
        return lax.rem(me_c + o, NC)

    def remote(src, dst, ssem, rsem, axis, target):
        return pltpu.make_async_remote_copy(
            src_ref=src, dst_ref=dst, send_sem=ssem, recv_sem=rsem, device_id={axis: target}, device_id_type=MESH
        )

    loads = [
        pltpu.make_async_copy(mq_hbm.at[me_h], rx.at[me_h], load_sem.at[0]),
        pltpu.make_async_copy(lse_hbm, lse_all.at[me_h], load_sem.at[1]),
        pltpu.make_async_copy(iq_hbm.at[me_h], iqraw.at[me_h], load_sem.at[2]),
        pltpu.make_async_copy(iw_hbm, iw_all.at[me_h], load_sem.at[3]),
        pltpu.make_async_copy(ik_hbm, ik, load_sem.at[4]),
        pltpu.make_async_copy(lat_hbm, kt.at[pl.ds(0, LAT), :], load_sem.at[5]),
    ]
    for load in loads:
        load.start()

    barrier = pltpu.get_barrier_semaphore()
    for target in (sibling, next_c, prev_c):
        pl.semaphore_signal(barrier, inc=1, device_id={"context": target}, device_id_type=MESH)
    for o in range(1, NH):
        pl.semaphore_signal(barrier, inc=1, device_id={"heads": plane(o)}, device_id_type=MESH)
    kt[LAT:, :] = jnp.zeros((WIDE + DIM - LAT, KEYS), BF16)
    pl.semaphore_wait(barrier, NH + 2)

    def q_copy(o):
        to = plane(o)
        return remote(mq_hbm.at[to], rx.at[me_h], q_ssem.at[o], q_rsem.at[me_h], "heads", to)

    def l_copy(o):
        return remote(lse_hbm, lse_all.at[me_h], l_ssem.at[o], l_rsem.at[me_h], "heads", plane(o))

    def i_copy(o):
        to = plane(o)
        return remote(iq_hbm.at[to], iqraw.at[me_h], i_ssem.at[o], i_rsem.at[me_h], "heads", to)

    def w_copy(o):
        return remote(iw_hbm, iw_all.at[me_h], w_ssem.at[o], w_rsem.at[me_h], "heads", plane(o))

    for copy in (q_copy, l_copy, i_copy, w_copy):
        for o in range(1, NH):
            copy(o).start()

    def arrived(buffer, rsem):
        for o in range(1, NH):
            other = plane(o)
            remote(buffer.at[other], buffer.at[other], rsem.at[other], rsem.at[other], "heads", other).wait_recv()

    loads[0].wait()
    arrived(rx, q_rsem)
    groups = []
    for g in range(8):
        group = rx[2 * g : 2 * g + 2].astype(F32).reshape(ROWS, LAT)
        qpack[0, g] = group[:, :WIDE].astype(BF16)
        groups.append(group[:, WIDE:])
    for g in range(4):
        pair = jnp.concatenate([groups[g], groups[g + 4]], axis=1)
        qpack[0, 8, :, g * DIM : (g + 1) * DIM] = pair.astype(BF16)

    cuts = (pl.ds(0, 4), pl.ds(4, 5))

    def chain(i, part, long):
        source_slot = 0 if i == 1 else (slot_l(i - 1) if long else slot_r(i - 1))
        target_slot = slot_l(i) if long else slot_r(i)
        ssem, rsem = (zl_send, zl_recv) if long else (zs_send, zs_recv)
        return remote(
            qpack.at[source_slot, cuts[part]], qpack.at[target_slot, cuts[part]],
            ssem.at[i - 1, part], rsem.at[i - 1, part], "context", next_c if long else prev_c,
        )

    def to_sibling(slot):
        target = {0: 1, 14: 15}.get(slot, slot + 2)
        index = {0: 0, 14: 7}.get(slot, 1 + (slot - 2) // 4 * 2 + (slot - 2) % 4)
        return remote(qpack.at[slot], qpack.at[target], sib_send.at[index], sib_recv.at[index], "context", sibling)

    for part in range(2):
        chain(1, part, True).start()
        chain(1, part, False).start()
    to_sibling(0).start()

    def advance(i, part):
        chain(i, part, True).wait_recv()
        if i < 4:
            chain(i + 1, part, True).start()
            chain(i, part, False).wait_recv()
            if i < 3:
                chain(i + 1, part, False).start()
        if part == 1:
            to_sibling(slot_l(i)).start()
            if i < 4:
                to_sibling(slot_r(i)).start()

    def widen(first, count):
        for slot in range(first, first + count):
            for g in range(4):
                both = qpack[slot, 8, :, g * DIM : (g + 1) * DIM]
                qext[slot, g] = both
                qext[slot, g + 4] = pltpu.roll(both.astype(F32), REST, axis=1).astype(BF16)

    lane_r = lax.broadcasted_iota(jnp.int32, (HEADS, NC * ROWS), 1)

    def shifts():
        table = lse_all[...].reshape(HEADS, NC * ROWS) * log2e
        for slot in range(16):
            picked = jnp.where(lane_r == source[slot] * ROWS + me_h, table, 0.0)
            lseb[slot] = jnp.broadcast_to(jnp.sum(picked, axis=1, keepdims=True), (HEADS, DIM))

    def piece(first, count, low, high):
        def one_tile(i, carry):
            at = pl.ds(pl.multiple_of(i * BIG, BIG), BIG)
            q_all = jnp.concatenate(
                [
                    qpack[first : first + count, :8].reshape(count * HEADS, WIDE),
                    qext[first : first + count].reshape(count * HEADS, DIM),
                ],
                axis=1,
            )
            score = jnp.dot(q_all, kt[:, at], preferred_element_type=F32)
            shift = lseb[first : first + count].reshape(count * HEADS, DIM)
            shift = jnp.concatenate([shift] * (BIG // DIM), axis=1)
            each = jnp.exp2(score * (main_scale * log2e) - shift)
            for b in range(count):
                row = jnp.sum(each[b * HEADS : (b + 1) * HEADS], axis=0, keepdims=True)
                mass[pl.ds(source[first + b], 1), at] = row
            return carry

        lax.fori_loop(low, high, one_tile, 0)

    loads[4].wait()
    for i in range(KEYS // DIM):
        at = pl.ds(i * DIM, DIM)
        ikt[:, at] = jnp.swapaxes(ik[at, :].astype(F32), 0, 1).astype(BF16)
    loads[1].wait()
    arrived(lse_all, l_rsem)
    shifts()
    loads[2].wait()
    arrived(iqraw, i_rsem)
    loads[3].wait()
    arrived(iw_all, w_rsem)
    qf[...] = iqraw[...].astype(F32)
    index_scale = DIM ** (-0.5)
    row_w = lax.broadcasted_iota(jnp.int32, (NC, ROWS, IDXH), 1)
    weights = jnp.sum(jnp.where(row_w == me_h, iw_all[...], 0.0), axis=1) * index_scale
    for j in range(IDXH):
        qjm[pl.ds(j * ROWS, ROWS), :] = qf[:, j, :].astype(BF16)
        wb[pl.ds(j * ROWS, ROWS), :] = jnp.broadcast_to(weights[:, j : j + 1], (ROWS, DIM))

    advance(1, 0)

    for i in range(IDXH * ROWS // DIM):
        at = pl.ds(i * DIM, DIM)
        qt[:, at] = jnp.swapaxes(qjm[at, :].astype(F32), 0, 1).astype(BF16)

    first_key = me_c * KEYS
    row_of = lax.broadcasted_iota(jnp.int32, (ROWS, BIG), 0)
    lane_of = lax.broadcasted_iota(jnp.int32, (ROWS, BIG), 1)
    limit = jnp.zeros((ROWS, BIG), jnp.int32)
    for c in range(NC):
        limit = jnp.where(row_of == c, len_ref[c * ROWS + me_h], limit)
    limit = limit - first_key - lane_of

    def visible(i):
        return i * BIG < limit

    def logits_tile(i, top):
        at = pl.ds(pl.multiple_of(i * BIG, BIG), BIG)
        k_tile = ikt[:, at]
        total = jnp.zeros((ROWS, BIG), F32)
        for r in range(4):
            rows = pl.ds(r * TILE, TILE)
            dots = jnp.maximum(jnp.dot(qjm[rows, :], k_tile, preferred_element_type=F32), 0.0)
            weight = jnp.concatenate([wb[rows, :]] * (BIG // DIM), axis=1)
            total = total + jnp.sum((dots * weight).reshape(TILE // ROWS, ROWS, BIG), axis=0)
        logits[:, at] = total
        return jnp.maximum(top, jnp.where(visible(i), total, masked_low))

    top = lax.fori_loop(0, KEYS // BIG, logits_tile, jnp.full((ROWS, BIG), masked_low, F32))
    own_top = jnp.max(top, axis=1, keepdims=True)

    def share_tile(i, total):
        at = pl.ds(pl.multiple_of(i * BIG, BIG), BIG)
        return total + jnp.where(visible(i), jnp.exp(logits[:, at] - own_top), 0.0)

    own_share = jnp.sum(
        lax.fori_loop(0, KEYS // BIG, share_tile, jnp.zeros((ROWS, BIG), F32)), axis=1, keepdims=True
    )

    loads[5].wait()
    advance(1, 1)
    to_sibling(0).wait_recv()
    widen(0, 2)
    piece(0, 2, 0, 4)
    for i in range(2, 5):
        advance(i, 0)
        to_sibling(slot_l(i - 1)).wait_recv()
        to_sibling(slot_r(i - 1)).wait_recv()
        widen(slot_l(i - 1), 4)
        piece(slot_l(i - 1), 4, 0, 2)
        advance(i, 1)
        piece(slot_l(i - 1), 4, 2, 4)
    to_sibling(14).wait_recv()
    widen(14, 2)
    piece(14, 2, 0, 4)

    def mass_tile(i, total):
        at = pl.ds(pl.multiple_of(i * BIG, BIG), BIG)
        seen = jnp.where(visible(i), mass[:, at], 0.0)
        mass[:, at] = seen
        return total + seen

    own_total = jnp.sum(
        lax.fori_loop(0, KEYS // BIG, mass_tile, jnp.zeros((ROWS, BIG), F32)), axis=1, keepdims=True
    )

    row_s = lax.broadcasted_iota(jnp.int32, (ROWS, DIM), 0)
    lane_s = lax.broadcasted_iota(jnp.int32, (ROWS, DIM), 1)
    packed = jnp.where(lane_s == row_s, own_top, 0.0)
    packed = jnp.where(lane_s == row_s + ROWS, own_share, packed)
    packed = jnp.where(lane_s == row_s + 2 * ROWS, own_total, packed)
    packed = jnp.sum(packed, axis=0, keepdims=True)
    st_send[...] = packed
    st_recv[me_c] = packed

    def stat_copy(o):
        return remote(st_send, st_recv.at[me_c], st_ssem.at[o], st_rsem.at[me_c], "context", line(o))

    for o in range(1, NC):
        stat_copy(o).start()

    def arrived_line(buffer, rsem):
        for o in range(1, NC):
            other = line(o)
            remote(buffer.at[other], buffer.at[other], rsem.at[other], rsem.at[other], "context", other).wait_recv()

    arrived_line(st_recv, st_rsem)

    stats = jnp.concatenate([st_recv[c] for c in range(NC)], axis=0)
    top_row = jnp.max(stats, axis=0, keepdims=True)
    share_row = jnp.sum(pltpu.roll(stats, DIM - ROWS, axis=1) * jnp.exp(stats - top_row), axis=0, keepdims=True)
    total_row = jnp.sum(pltpu.roll(stats, DIM - 2 * ROWS, axis=1), axis=0, keepdims=True)

    def column_of(row):
        wide = jnp.broadcast_to(row, (ROWS, DIM))
        return jnp.sum(jnp.where(lane_s == row_s, wide, 0.0), axis=1, keepdims=True)

    top_col = column_of(top_row)
    share_col = loss_scale / column_of(share_row)
    total_col = loss_scale / column_of(total_row)

    def slope_tile(i, carry):
        at = pl.ds(pl.multiple_of(i * BIG, BIG), BIG)
        chance = jnp.where(visible(i), jnp.exp(logits[:, at] - top_col), 0.0)
        mass[:, at] = chance * share_col - mass[:, at] * total_col
        return carry

    lax.fori_loop(0, KEYS // BIG, slope_tile, 0)

    def gq_copy(owner):
        return remote(gq_send.at[owner], gq_recv.at[me_c], gq_ssem.at[owner], gq_rsem.at[me_c], "context", owner)

    def query_rows(i, carry):
        chunk = lax.rem(me_c // 4 + 1 + i, 4)
        rows = pl.ds(pl.multiple_of(chunk * TILE, TILE), TILE)
        weight = jnp.concatenate([wb[rows, :]] * (BIG // DIM), axis=1).reshape(TILE // ROWS, ROWS, BIG)

        def term_tile(t, inner):
            at = pl.ds(pl.multiple_of(t * BIG, BIG), BIG)
            dots = jnp.dot(qjm[rows, :], ikt[:, at], preferred_element_type=F32).reshape(TILE // ROWS, ROWS, BIG)
            term = jnp.where(dots > 0, mass[:, at][None] * weight, 0.0)
            terms[rows, at] = term.reshape(TILE, BIG).astype(BF16)
            return inner

        lax.fori_loop(0, KEYS // BIG, term_tile, 0)
        grad = jnp.dot(terms[rows, :], ik[...], preferred_element_type=F32)
        for b in range(4):
            owner = chunk * 4 + b
            part = grad[b * 64 : (b + 1) * 64, :]
            gq_send[owner] = part.astype(BF16)

            @pl.when(owner != me_c)
            def _():
                gq_copy(owner).start()

            @pl.when(owner == me_c)
            def _():
                gq_own[...] = part

        return carry

    lax.fori_loop(0, 4, query_rows, 0)

    def gk_copy(owner):
        return remote(gk_send.at[owner], gk_recv.at[me_h], gk_ssem.at[owner], gk_rsem.at[me_h], "heads", owner)

    def key_tile(i, carry):
        quad = lax.rem(me_h // 4 + 1 + i, 4)
        at = pl.ds(pl.multiple_of(quad * BIG, BIG), BIG)
        grad = jnp.dot(qt[...], terms[:, at], preferred_element_type=F32)
        for b in range(4):
            owner = quad * 4 + b
            part = grad[:, b * DIM : (b + 1) * DIM]
            gk_send[owner] = part.astype(BF16)

            @pl.when(owner != me_h)
            def _():
                gk_copy(owner).start()

            @pl.when(owner == me_h)
            def _():
                gk_own[...] = part

        return carry

    lax.fori_loop(0, 4, key_tile, 0)

    arrived_line(gq_recv, gq_rsem)
    query_sum = gq_own[...]
    for o in range(1, NC):
        query_sum = query_sum + gq_recv[line(o)].astype(F32)
    for j in range(IDXH // NC):
        fin_send[:, j, :] = query_sum[j * ROWS : (j + 1) * ROWS, :]

    def fin_copy(o):
        to = plane(o)
        return remote(fin_send.at[to], fin_recv.at[me_h], fin_ssem.at[o], fin_rsem.at[me_h], "heads", to)

    for o in range(1, NH):
        fin_copy(o).start()
    fin_recv[me_h] = fin_send[me_h]

    arrived(gk_recv, gk_rsem)
    key_sum = gk_own[...]
    for o in range(1, NH):
        key_sum = key_sum + gk_recv[plane(o)].astype(F32)
    ok_ref[...] = jnp.swapaxes(key_sum, 0, 1)

    arrived(fin_recv, fin_rsem)
    oq_ref[...] = fin_recv[...]

    for part in range(2):
        for i in range(1, 5):
            chain(i, part, True).wait_send()
        for i in range(1, 4):
            chain(i, part, False).wait_send()
    for slot in (0, 2, 3, 6, 7, 10, 11, 14):
        to_sibling(slot).wait_send()
    for o in range(1, NC):
        for copy in (q_copy, l_copy, i_copy, w_copy, stat_copy, fin_copy):
            copy(o).wait_send()
        gk_copy(plane(o)).wait_send()
        gq_copy(line(o)).wait_send()


def on_device(main_query, latent_keys, head_lse, lengths, index_query, index_key, index_weight):
    hbm = pl.BlockSpec(memory_space=pl.ANY)
    vmem = pl.BlockSpec(memory_space=pltpu.VMEM)
    smem = pl.BlockSpec(memory_space=pltpu.SMEM)
    dma = pltpu.SemaphoreType.DMA
    return pl.pallas_call(
        kernel,
        out_shape=(
            jax.ShapeDtypeStruct((ROWS, IDXH // NC, DIM), F32),
            jax.ShapeDtypeStruct((KEYS // NH, DIM), F32),
        ),
        in_specs=[hbm, hbm, hbm, smem, hbm, hbm, hbm],
        out_specs=(vmem, vmem),
        scratch_shapes=[
            pltpu.VMEM((NH, HL, LAT), BF16),
            pltpu.VMEM((16, 9, ROWS, WIDE), BF16),
            pltpu.VMEM((16, 8, ROWS, DIM), BF16),
            pltpu.VMEM((NH, HL, NC * ROWS), F32),
            pltpu.VMEM((16, HEADS, DIM), F32),
            pltpu.VMEM((WIDE + DIM, KEYS), BF16),
            pltpu.VMEM((NH, IDXH, DIM), BF16),
            pltpu.VMEM((NH, IDXH, DIM), F32),
            pltpu.VMEM((IDXH * ROWS, DIM), BF16),
            pltpu.VMEM((DIM, IDXH * ROWS), BF16),
            pltpu.VMEM((NH, ROWS, IDXH), F32),
            pltpu.VMEM((IDXH * ROWS, DIM), F32),
            pltpu.VMEM((KEYS, DIM), BF16),
            pltpu.VMEM((DIM, KEYS), BF16),
            pltpu.VMEM((ROWS, KEYS), F32),
            pltpu.VMEM((ROWS, KEYS), F32),
            pltpu.VMEM((1, DIM), F32),
            pltpu.VMEM((NC, 1, DIM), F32),
            pltpu.VMEM((IDXH * ROWS, KEYS), BF16),
            pltpu.VMEM((NH, DIM, DIM), BF16),
            pltpu.VMEM((NH, DIM, DIM), BF16),
            pltpu.VMEM((DIM, DIM), F32),
            pltpu.VMEM((NC, 64, DIM), BF16),
            pltpu.VMEM((NC, 64, DIM), BF16),
            pltpu.VMEM((64, DIM), F32),
            pltpu.VMEM((NH, IDXH // NC, DIM), F32),
            pltpu.VMEM((NH, IDXH // NC, DIM), F32),
            dma((6,)),
            *[dma((16,))] * 8,
            dma((4, 2)),
            dma((4, 2)),
            dma((3, 2)),
            dma((3, 2)),
            dma((8,)),
            dma((8,)),
            *[dma((16,))] * 8,
        ],
        compiler_params=pltpu.CompilerParams(
            collective_id=0, has_side_effects=True, vmem_limit_bytes=56 * 1024 * 1024
        ),
        name="index_grads",
    )(main_query, latent_keys.T, head_lse.T, lengths, index_query, index_key, index_weight)


def solution(mesh):
    placed = (
        P("context", "heads", None),
        P("context", None),
        P(None, "heads"),
        P(),
        P("heads", None, None),
        P("context", None),
        P("heads", None),
    )
    return jax.shard_map(
        on_device,
        mesh=mesh,
        in_specs=placed,
        out_specs=(P("heads", "context", None), P(("context", "heads"), None)),
        check_vma=False,
    )
```

time: 376 us -> 67.4 us (0.18)
  waiting for transfers between devices: 232 us -> 0 us
  Pallas kernels: 0 us -> 63.7 us
  blocking collectives: 48.6 us -> 0 us
  matrix products: 46.5 us -> 0 us
  local copies, waits for them, and re-layouts: 26.6 us -> 2.85 us
  between operations: 13.8 us -> 0.64 us
  other arithmetic: 6.2 us -> 0 us
    reduce_scatter x2 -> x0, waiting for transfers between devices: 135 us -> none  [the longest x1 81.3 us: on_device(): lax.psum_scatter(key_grad, 'heads', scatter_dimension=0, tiled=True)]
    pallas_call x0 -> x1, Pallas kernels: none -> 63.7 us  [on_device(): pl.pallas_call(kernel, out_shape=(jax.ShapeDtypeStruct((ROWS, IDXH // NC,...]
    psum x1 -> x0, waiting for transfers between devices: 53.3 us -> none  [on_device(): summed_mass = lax.psum(partial_mass, 'heads')]
    dot_general x24 -> x0, matrix products: 46.5 us -> none  [the longest x4 19.1 us: one_block(): jnp.einsum('rhd,sd->rhs', query_block, latent, preferred_element_type=jnp...]
    all_gather x1 -> x0, waiting for transfers between devices: 43 us -> none  [on_device(): lax.all_gather(main_query, 'context', axis=0, tiled=True)]
    psum x1 -> x0, blocking collectives: 25.4 us -> none  [on_device(): lax.psum((jnp.sum(weights_exp, axis=1), mass_local), 'context')]
    pmax x1 -> x0, blocking collectives: 23.3 us -> none  [on_device(): top = lax.pmax(local_top, 'context')]
    mul x13 -> x0, local copies, waits for them, and re-layouts: 12.1 us -> none  [back_step(): slope_block[:, None, :] * index_weight[:, :, None] * index_scale]
  transfers between devices with their start and end apart: 4 -> 0, of which waited for: 4 -> 0; matrix products, arithmetic and copies ran while one was open for 7% -> 0% of each run, Pallas kernels for 0% -> 0%
where the time goes in v1:
time: 67.4 us; the launch traced here: 67.2 us
  Pallas kernels  63.7 us (95%)
  local copies, waits for them, and re-layouts  2.85 us (4%)
    pallas_call x1, Pallas kernels, on_device(): pl.pallas_call(kernel, out_shape=(jax.ShapeDtypeStruct((ROWS, IDXH // NC,...  63.7 us
    unnamed x2, local copies, waits for them, and re-layouts  2.85 us

profile of v1, /device:TPU:1, one launch (start us, length us, event | category | flops | bytes accessed | tf_op | source)
XLA Modules:
  0.0 67.2 jit_solution(8142800675349854900)
XLA Ops:
  0.6 63.7 %index_grads.1 = (f32[16,4,128]{2,1,0:T(4,128)}, f32[128,128]{1,0:T(8,128)}) custom-call(bf16[16,8,576]{2,1,0:T(8,128)(2,1)} %mq_hbm.1, bf16[576,2048]{1,0:T(8,128)(2,1)} %bitcast.2, f32[8,256]{1,0:T(8,128)} %bitcast.3, s32[256]{0:T(256)} %len_ref.1, bf16[16,64,128]{2,1,0:T(8,128)(2,1)} %iq_hbm.1, bf16[2048,128]{1,0:T(8,128)(2,1)} %ik_hbm.1, f32[16,64]{1,0:T(8,128)} %iw_hbm.1), custom_call_target="tpu_custom_call" | custom-call | tf_op jit(solution)/shard_map/index_grads/pallas_call | solution.py:435
  64.3 1.4 %copy.11 = f32[16,4,128]{2,1,0:T(4,128)} copy(f32[16,4,128]{2,1,0:T(4,128)} %get-tuple-element.4) | data formatting | bytes 65536
  65.7 1.5 %copy.12 = f32[128,128]{1,0:T(8,128)} copy(f32[128,128]{1,0:T(8,128)} %get-tuple-element.5) | data formatting | bytes 131072

commit v2 on v1

--- a/solution.py
+++ b/solution.py
@@ -42,11 +42,11 @@
 
 def kernel(
     mq_hbm, lat_hbm, lse_hbm, len_ref, iq_hbm, ik_hbm, iw_hbm, oq_ref, ok_ref,
-    rx, qpack, qext, lse_all, lseb, kt, iqraw, qf, qjm, qt, iw_all, wb, ik, ikt, logits, mass,
-    st_send, st_recv, terms, gk_send, gk_recv, gk_own, gq_send, gq_recv, gq_own, fin_send, fin_recv,
-    load_sem, q_ssem, q_rsem, l_ssem, l_rsem, i_ssem, i_rsem, w_ssem, w_rsem,
+    qraw, rx, qpack, qext, lse_all, lseb, kt, iqraw, qf, qjm, qt, iwv, wb, ik, ikt, wm, logits, mass, msend, mrecv,
+    st_send, st_recv, terms, gk_send, gk_recv, gk_own, gq_send, gq_recv, gq_own,
+    load_sem, q_ssem, q_rsem, l_ssem, l_rsem, m_ssem, m_rsem,
     zl_send, zl_recv, zs_send, zs_recv, sib_send, sib_recv, st_ssem, st_rsem,
-    gk_ssem, gk_rsem, gq_ssem, gq_rsem, fin_ssem, fin_rsem,
+    gk_ssem, gk_rsem, gq_ssem, gq_rsem,
 ):
     me_c = lax.axis_index("context")
     me_h = lax.axis_index("heads")
@@ -81,10 +81,10 @@
         )
 
     loads = [
-        pltpu.make_async_copy(mq_hbm.at[me_h], rx.at[me_h], load_sem.at[0]),
+        pltpu.make_async_copy(mq_hbm, qraw, load_sem.at[0]),
         pltpu.make_async_copy(lse_hbm, lse_all.at[me_h], load_sem.at[1]),
-        pltpu.make_async_copy(iq_hbm.at[me_h], iqraw.at[me_h], load_sem.at[2]),
-        pltpu.make_async_copy(iw_hbm, iw_all.at[me_h], load_sem.at[3]),
+        pltpu.make_async_copy(iq_hbm, iqraw, load_sem.at[2]),
+        pltpu.make_async_copy(iw_hbm, iwv, load_sem.at[3]),
         pltpu.make_async_copy(ik_hbm, ik, load_sem.at[4]),
         pltpu.make_async_copy(lat_hbm, kt.at[pl.ds(0, LAT), :], load_sem.at[5]),
     ]
@@ -97,23 +97,29 @@
     for o in range(1, NH):
         pl.semaphore_signal(barrier, inc=1, device_id={"heads": plane(o)}, device_id_type=MESH)
     kt[LAT:, :] = jnp.zeros((WIDE + DIM - LAT, KEYS), BF16)
+    loads[0].wait()
+    rx[me_h] = qraw[me_h]
+    loads[4].wait()
+    for i in range(KEYS // DIM):
+        at = pl.ds(i * DIM, DIM)
+        ikt[:, at] = jnp.swapaxes(ik[at, :].astype(F32), 0, 1).astype(BF16)
+    loads[2].wait()
+    loads[3].wait()
+    qf[...] = iqraw[...].astype(F32)
+    weights = iwv[...] * DIM ** (-0.5)
+    for j in range(IDXH):
+        qjm[pl.ds(j * ROWS, ROWS), :] = qf[:, j, :].astype(BF16)
+        wb[pl.ds(j * ROWS, ROWS), :] = jnp.broadcast_to(weights[:, j : j + 1], (ROWS, DIM))
     pl.semaphore_wait(barrier, NH + 2)
 
     def q_copy(o):
         to = plane(o)
-        return remote(mq_hbm.at[to], rx.at[me_h], q_ssem.at[o], q_rsem.at[me_h], "heads", to)
+        return remote(qraw.at[to], rx.at[me_h], q_ssem.at[o], q_rsem.at[me_h], "heads", to)
 
     def l_copy(o):
         return remote(lse_hbm, lse_all.at[me_h], l_ssem.at[o], l_rsem.at[me_h], "heads", plane(o))
 
-    def i_copy(o):
-        to = plane(o)
-        return remote(iq_hbm.at[to], iqraw.at[me_h], i_ssem.at[o], i_rsem.at[me_h], "heads", to)
-
-    def w_copy(o):
-        return remote(iw_hbm, iw_all.at[me_h], w_ssem.at[o], w_rsem.at[me_h], "heads", plane(o))
-
-    for copy in (q_copy, l_copy, i_copy, w_copy):
+    for copy in (q_copy, l_copy):
         for o in range(1, NH):
             copy(o).start()
 
@@ -122,7 +128,42 @@
             other = plane(o)
             remote(buffer.at[other], buffer.at[other], rsem.at[other], rsem.at[other], "heads", other).wait_recv()
 
-    loads[0].wait()
+    first_key = me_c * KEYS
+    row_of = lax.broadcasted_iota(jnp.int32, (ROWS, BIG), 0)
+    lane_of = lax.broadcasted_iota(jnp.int32, (ROWS, BIG), 1)
+    limit = jnp.zeros((ROWS, BIG), jnp.int32)
+    for t in range(ROWS):
+        limit = jnp.where(row_of == t, len_ref[me_h * ROWS + t], limit)
+    limit = limit - first_key - lane_of
+
+    def visible(i):
+        return i * BIG < limit
+
+    def logits_tile(i, top):
+        at = pl.ds(pl.multiple_of(i * BIG, BIG), BIG)
+        k_tile = ikt[:, at]
+        total = jnp.zeros((ROWS, BIG), F32)
+        for r in range(4):
+            rows = pl.ds(r * TILE, TILE)
+            dots = jnp.dot(qjm[rows, :], k_tile, preferred_element_type=F32)
+            weight = jnp.concatenate([wb[rows, :]] * (BIG // DIM), axis=1)
+            masked = jnp.where(dots > 0, weight, 0.0)
+            wm[rows, at] = masked
+            total = total + jnp.sum((dots * masked).reshape(TILE // ROWS, ROWS, BIG), axis=0)
+        logits[:, at] = total
+        return jnp.maximum(top, jnp.where(visible(i), total, masked_low))
+
+    top = lax.fori_loop(0, KEYS // BIG, logits_tile, jnp.full((ROWS, BIG), masked_low, F32))
+    own_top = jnp.max(top, axis=1, keepdims=True)
+
+    def share_tile(i, total):
+        at = pl.ds(pl.multiple_of(i * BIG, BIG), BIG)
+        return total + jnp.where(visible(i), jnp.exp(logits[:, at] - own_top), 0.0)
+
+    own_share = jnp.sum(
+        lax.fori_loop(0, KEYS // BIG, share_tile, jnp.zeros((ROWS, BIG), F32)), axis=1, keepdims=True
+    )
+
     arrived(rx, q_rsem)
     groups = []
     for g in range(8):
@@ -172,6 +213,21 @@
                 both = qpack[slot, 8, :, g * DIM : (g + 1) * DIM]
                 qext[slot, g] = both
                 qext[slot, g + 4] = pltpu.roll(both.astype(F32), REST, axis=1).astype(BF16)
+
+    def mass_copy(slot):
+        to = source[slot]
+        return remote(msend.at[to], mrecv.at[me_h], m_ssem.at[slot], m_rsem.at[me_h], "heads", to)
+
+    def deliver(first, count):
+        for slot in range(first, first + count):
+
+            @pl.when(source[slot] != me_h)
+            def _():
+                mass_copy(slot).start()
+
+            @pl.when(source[slot] == me_h)
+            def _():
+                mrecv[me_h] = msend[me_h]
 
     lane_r = lax.broadcasted_iota(jnp.int32, (HEADS, NC * ROWS), 1)
 
@@ -197,90 +253,57 @@
             each = jnp.exp2(score * (main_scale * log2e) - shift)
             for b in range(count):
                 row = jnp.sum(each[b * HEADS : (b + 1) * HEADS], axis=0, keepdims=True)
-                mass[pl.ds(source[first + b], 1), at] = row
+                msend[source[first + b], :, at] = row
             return carry
 
         lax.fori_loop(low, high, one_tile, 0)
 
-    loads[4].wait()
-    for i in range(KEYS // DIM):
-        at = pl.ds(i * DIM, DIM)
-        ikt[:, at] = jnp.swapaxes(ik[at, :].astype(F32), 0, 1).astype(BF16)
+    def siblings_of(i):
+        to_sibling(slot_l(i)).wait_recv()
+        to_sibling(slot_r(i)).wait_recv()
+        widen(slot_l(i), 4)
+
     loads[1].wait()
     arrived(lse_all, l_rsem)
     shifts()
-    loads[2].wait()
-    arrived(iqraw, i_rsem)
-    loads[3].wait()
-    arrived(iw_all, w_rsem)
-    qf[...] = iqraw[...].astype(F32)
-    index_scale = DIM ** (-0.5)
-    row_w = lax.broadcasted_iota(jnp.int32, (NC, ROWS, IDXH), 1)
-    weights = jnp.sum(jnp.where(row_w == me_h, iw_all[...], 0.0), axis=1) * index_scale
-    for j in range(IDXH):
-        qjm[pl.ds(j * ROWS, ROWS), :] = qf[:, j, :].astype(BF16)
-        wb[pl.ds(j * ROWS, ROWS), :] = jnp.broadcast_to(weights[:, j : j + 1], (ROWS, DIM))
-
     advance(1, 0)
-
+    advance(1, 1)
+    loads[5].wait()
+    to_sibling(0).wait_recv()
+    widen(0, 2)
+    piece(0, 2, 0, 4)
+    deliver(0, 2)
+    advance(2, 0)
     for i in range(IDXH * ROWS // DIM):
         at = pl.ds(i * DIM, DIM)
         qt[:, at] = jnp.swapaxes(qjm[at, :].astype(F32), 0, 1).astype(BF16)
-
-    first_key = me_c * KEYS
-    row_of = lax.broadcasted_iota(jnp.int32, (ROWS, BIG), 0)
-    lane_of = lax.broadcasted_iota(jnp.int32, (ROWS, BIG), 1)
-    limit = jnp.zeros((ROWS, BIG), jnp.int32)
-    for c in range(NC):
-        limit = jnp.where(row_of == c, len_ref[c * ROWS + me_h], limit)
-    limit = limit - first_key - lane_of
-
-    def visible(i):
-        return i * BIG < limit
-
-    def logits_tile(i, top):
-        at = pl.ds(pl.multiple_of(i * BIG, BIG), BIG)
-        k_tile = ikt[:, at]
-        total = jnp.zeros((ROWS, BIG), F32)
-        for r in range(4):
-            rows = pl.ds(r * TILE, TILE)
-            dots = jnp.maximum(jnp.dot(qjm[rows, :], k_tile, preferred_element_type=F32), 0.0)
-            weight = jnp.concatenate([wb[rows, :]] * (BIG // DIM), axis=1)
-            total = total + jnp.sum((dots * weight).reshape(TILE // ROWS, ROWS, BIG), axis=0)
-        logits[:, at] = total
-        return jnp.maximum(top, jnp.where(visible(i), total, masked_low))
-
-    top = lax.fori_loop(0, KEYS // BIG, logits_tile, jnp.full((ROWS, BIG), masked_low, F32))
-    own_top = jnp.max(top, axis=1, keepdims=True)
-
-    def share_tile(i, total):
-        at = pl.ds(pl.multiple_of(i * BIG, BIG), BIG)
-        return total + jnp.where(visible(i), jnp.exp(logits[:, at] - own_top), 0.0)
-
-    own_share = jnp.sum(
-        lax.fori_loop(0, KEYS // BIG, share_tile, jnp.zeros((ROWS, BIG), F32)), axis=1, keepdims=True
-    )
-
-    loads[5].wait()
-    advance(1, 1)
-    to_sibling(0).wait_recv()
-    widen(0, 2)
-    piece(0, 2, 0, 4)
-    for i in range(2, 5):
-        advance(i, 0)
-        to_sibling(slot_l(i - 1)).wait_recv()
-        to_sibling(slot_r(i - 1)).wait_recv()
-        widen(slot_l(i - 1), 4)
-        piece(slot_l(i - 1), 4, 0, 2)
-        advance(i, 1)
-        piece(slot_l(i - 1), 4, 2, 4)
+    advance(2, 1)
+    siblings_of(1)
+    piece(slot_l(1), 4, 0, 3)
+    advance(3, 0)
+    piece(slot_l(1), 4, 3, 4)
+    deliver(slot_l(1), 4)
+    advance(3, 1)
+    siblings_of(2)
+    piece(slot_l(2), 4, 0, 3)
+    advance(4, 0)
+    piece(slot_l(2), 4, 3, 4)
+    deliver(slot_l(2), 4)
+    siblings_of(3)
+    piece(slot_l(3), 4, 0, 2)
+    advance(4, 1)
+    piece(slot_l(3), 4, 2, 4)
+    deliver(slot_l(3), 4)
     to_sibling(14).wait_recv()
     widen(14, 2)
     piece(14, 2, 0, 4)
+    deliver(14, 2)
+
+    arrived(mrecv, m_rsem)
 
     def mass_tile(i, total):
         at = pl.ds(pl.multiple_of(i * BIG, BIG), BIG)
-        seen = jnp.where(visible(i), mass[:, at], 0.0)
+        seen = jnp.where(visible(i), jnp.concatenate([mrecv[t, :, at] for t in range(ROWS)], axis=0), 0.0)
         mass[:, at] = seen
         return total + seen
 
@@ -331,46 +354,17 @@
 
     lax.fori_loop(0, KEYS // BIG, slope_tile, 0)
 
-    def gq_copy(owner):
-        return remote(gq_send.at[owner], gq_recv.at[me_c], gq_ssem.at[owner], gq_rsem.at[me_c], "context", owner)
-
-    def query_rows(i, carry):
-        chunk = lax.rem(me_c // 4 + 1 + i, 4)
-        rows = pl.ds(pl.multiple_of(chunk * TILE, TILE), TILE)
-        weight = jnp.concatenate([wb[rows, :]] * (BIG // DIM), axis=1).reshape(TILE // ROWS, ROWS, BIG)
-
-        def term_tile(t, inner):
-            at = pl.ds(pl.multiple_of(t * BIG, BIG), BIG)
-            dots = jnp.dot(qjm[rows, :], ikt[:, at], preferred_element_type=F32).reshape(TILE // ROWS, ROWS, BIG)
-            term = jnp.where(dots > 0, mass[:, at][None] * weight, 0.0)
-            terms[rows, at] = term.reshape(TILE, BIG).astype(BF16)
-            return inner
-
-        lax.fori_loop(0, KEYS // BIG, term_tile, 0)
-        grad = jnp.dot(terms[rows, :], ik[...], preferred_element_type=F32)
-        for b in range(4):
-            owner = chunk * 4 + b
-            part = grad[b * 64 : (b + 1) * 64, :]
-            gq_send[owner] = part.astype(BF16)
-
-            @pl.when(owner != me_c)
-            def _():
-                gq_copy(owner).start()
-
-            @pl.when(owner == me_c)
-            def _():
-                gq_own[...] = part
-
-        return carry
-
-    lax.fori_loop(0, 4, query_rows, 0)
-
     def gk_copy(owner):
         return remote(gk_send.at[owner], gk_recv.at[me_h], gk_ssem.at[owner], gk_rsem.at[me_h], "heads", owner)
 
     def key_tile(i, carry):
         quad = lax.rem(me_h // 4 + 1 + i, 4)
         at = pl.ds(pl.multiple_of(quad * BIG, BIG), BIG)
+        slope = mass[:, at][None]
+        for r in range(4):
+            rows = pl.ds(r * TILE, TILE)
+            term = wm[rows, at].reshape(TILE // ROWS, ROWS, BIG) * slope
+            terms[rows, at] = term.reshape(TILE, BIG).astype(BF16)
         grad = jnp.dot(qt[...], terms[:, at], preferred_element_type=F32)
         for b in range(4):
             owner = quad * 4 + b
@@ -389,29 +383,42 @@
 
     lax.fori_loop(0, 4, key_tile, 0)
 
+    def gq_copy(owner):
+        return remote(gq_send.at[owner], gq_recv.at[me_c], gq_ssem.at[owner], gq_rsem.at[me_c], "context", owner)
+
+    def query_rows(i, carry):
+        chunk = lax.rem(me_c // 2 + 4 + (1 - 2 * lax.rem(i, 2)) * ((i + 1) // 2), 8)
+        rows = pl.ds(pl.multiple_of(chunk * DIM, DIM), DIM)
+        grad = jnp.dot(terms[rows, :], ik[...], preferred_element_type=F32)
+        for b in range(2):
+            owner = chunk * 2 + b
+            part = grad[b * 64 : (b + 1) * 64, :]
+            gq_send[owner] = part.astype(BF16)
+
+            @pl.when(owner != me_c)
+            def _():
+                gq_copy(owner).start()
+
+            @pl.when(owner == me_c)
+            def _():
+                gq_own[...] = part
+
+        return carry
+
+    lax.fori_loop(0, 8, query_rows, 0)
+
+    arrived(gk_recv, gk_rsem)
+    key_sum = gk_own[...]
+    for o in range(1, NH):
+        key_sum = key_sum + gk_recv[plane(o)].astype(F32)
+    ok_ref[...] = jnp.swapaxes(key_sum, 0, 1)
+
     arrived_line(gq_recv, gq_rsem)
     query_sum = gq_own[...]
     for o in range(1, NC):
         query_sum = query_sum + gq_recv[line(o)].astype(F32)
     for j in range(IDXH // NC):
-        fin_send[:, j, :] = query_sum[j * ROWS : (j + 1) * ROWS, :]
-
-    def fin_copy(o):
-        to = plane(o)
-        return remote(fin_send.at[to], fin_recv.at[me_h], fin_ssem.at[o], fin_rsem.at[me_h], "heads", to)
-
-    for o in range(1, NH):
-        fin_copy(o).start()
-    fin_recv[me_h] = fin_send[me_h]
-
-    arrived(gk_recv, gk_rsem)
-    key_sum = gk_own[...]
-    for o in range(1, NH):
-        key_sum = key_sum + gk_recv[plane(o)].astype(F32)
-    ok_ref[...] = jnp.swapaxes(key_sum, 0, 1)
-
-    arrived(fin_recv, fin_rsem)
-    oq_ref[...] = fin_recv[...]
+        oq_ref[:, j, :] = query_sum[j * ROWS : (j + 1) * ROWS, :]
 
     for part in range(2):
         for i in range(1, 5):
@@ -420,11 +427,22 @@
             chain(i, part, False).wait_send()
     for slot in (0, 2, 3, 6, 7, 10, 11, 14):
         to_sibling(slot).wait_send()
+    for slot in range(16):
+
+        @pl.when(source[slot] != me_h)
+        def _():
+            mass_copy(slot).wait_send()
+
     for o in range(1, NC):
-        for copy in (q_copy, l_copy, i_copy, w_copy, stat_copy, fin_copy):
+        for copy in (q_copy, l_copy, stat_copy):
             copy(o).wait_send()
         gk_copy(plane(o)).wait_send()
         gq_copy(line(o)).wait_send()
+
+
+def finish(query_ref, key_ref, oq_ref, ok_ref):
+    oq_ref[...] = query_ref[...]
+    ok_ref[...] = key_ref[...]
 
 
 def on_device(main_query, latent_keys, head_lse, lengths, index_query, index_key, index_weight):
@@ -432,7 +450,7 @@
     vmem = pl.BlockSpec(memory_space=pltpu.VMEM)
     smem = pl.BlockSpec(memory_space=pltpu.SMEM)
     dma = pltpu.SemaphoreType.DMA
-    return pl.pallas_call(
+    out_query, out_key = pl.pallas_call(
         kernel,
         out_shape=(
             jax.ShapeDtypeStruct((ROWS, IDXH // NC, DIM), F32),
@@ -441,6 +459,7 @@
         in_specs=[hbm, hbm, hbm, smem, hbm, hbm, hbm],
         out_specs=(vmem, vmem),
         scratch_shapes=[
+            pltpu.VMEM((ROWS, HL, LAT), BF16),
             pltpu.VMEM((NH, HL, LAT), BF16),
             pltpu.VMEM((16, 9, ROWS, WIDE), BF16),
             pltpu.VMEM((16, 8, ROWS, DIM), BF16),
@@ -451,12 +470,15 @@
             pltpu.VMEM((NH, IDXH, DIM), F32),
             pltpu.VMEM((IDXH * ROWS, DIM), BF16),
             pltpu.VMEM((DIM, IDXH * ROWS), BF16),
-            pltpu.VMEM((NH, ROWS, IDXH), F32),
+            pltpu.VMEM((ROWS, IDXH), F32),
             pltpu.VMEM((IDXH * ROWS, DIM), F32),
             pltpu.VMEM((KEYS, DIM), BF16),
             pltpu.VMEM((DIM, KEYS), BF16),
+            pltpu.VMEM((IDXH * ROWS, KEYS), F32),
             pltpu.VMEM((ROWS, KEYS), F32),
             pltpu.VMEM((ROWS, KEYS), F32),
+            pltpu.VMEM((16, 1, KEYS), F32),
+            pltpu.VMEM((NH, 1, KEYS), F32),
             pltpu.VMEM((1, DIM), F32),
             pltpu.VMEM((NC, 1, DIM), F32),
             pltpu.VMEM((IDXH * ROWS, KEYS), BF16),
@@ -466,23 +488,31 @@
             pltpu.VMEM((NC, 64, DIM), BF16),
             pltpu.VMEM((NC, 64, DIM), BF16),
             pltpu.VMEM((64, DIM), F32),
-            pltpu.VMEM((NH, IDXH // NC, DIM), F32),
-            pltpu.VMEM((NH, IDXH // NC, DIM), F32),
             dma((6,)),
-            *[dma((16,))] * 8,
+            *[dma((16,))] * 6,
             dma((4, 2)),
             dma((4, 2)),
             dma((3, 2)),
             dma((3, 2)),
             dma((8,)),
             dma((8,)),
-            *[dma((16,))] * 8,
+            *[dma((16,))] * 6,
         ],
         compiler_params=pltpu.CompilerParams(
             collective_id=0, has_side_effects=True, vmem_limit_bytes=56 * 1024 * 1024
         ),
         name="index_grads",
     )(main_query, latent_keys.T, head_lse.T, lengths, index_query, index_key, index_weight)
+    return pl.pallas_call(
+        finish,
+        out_shape=(
+            jax.ShapeDtypeStruct((ROWS, IDXH // NC, DIM), F32),
+            jax.ShapeDtypeStruct((KEYS // NH, DIM), F32),
+        ),
+        in_specs=[vmem, vmem],
+        out_specs=(vmem, vmem),
+        name="finish",
+    )(out_query, out_key)
 
 
 def solution(mesh):

time: 67.4 us -> 62.4 us (0.926)
  local copies, waits for them, and re-layouts: 2.85 us -> 0 us
  Pallas kernels: 63.7 us -> 61.6 us
    pallas_call x1, Pallas kernels: 63.7 us -> 60.1 us  [on_device(): pl.pallas_call(kernel, out_shape=(jax.ShapeDtypeStruct((ROWS, IDXH // NC,...]
    unnamed x2 -> x0, local copies, waits for them, and re-layouts: 2.85 us -> none
    pallas_call x0 -> x1, Pallas kernels: none -> 1.5 us  [on_device(): pl.pallas_call(finish, out_shape=(jax.ShapeDtypeStruct((ROWS, IDXH // NC,...]
where the time goes in v2:
time: 62.4 us; the launch traced here: 62.3 us
  Pallas kernels  61.6 us (99%)
  between operations  0.64 us (1%)
    pallas_call x1, Pallas kernels, on_device(): pl.pallas_call(kernel, out_shape=(jax.ShapeDtypeStruct((ROWS, IDXH // NC,...  60.1 us
    pallas_call x1, Pallas kernels, on_device(): pl.pallas_call(finish, out_shape=(jax.ShapeDtypeStruct((ROWS, IDXH // NC,...  1.5 us

profile of v2, /device:TPU:1, one launch (start us, length us, event | category | flops | bytes accessed | tf_op | source)
XLA Modules:
  0.0 62.3 jit_solution(5672856926090125532)
XLA Ops:
  0.6 60.1 %index_grads.1 = (f32[16,4,128]{2,1,0:T(4,128)}, f32[128,128]{1,0:T(8,128)}) custom-call(bf16[16,8,576]{2,1,0:T(8,128)(2,1)} %mq_hbm.1, bf16[576,2048]{1,0:T(8,128)(2,1)} %bitcast.2, f32[8,256]{1,0:T(8,128)} %bitcast.3, s32[256]{0:T(256)} %len_ref.1, bf16[16,64,128]{2,1,0:T(8,128)(2,1)} %iq_hbm.1, bf16[2048,128]{1,0:T(8,128)(2,1)} %ik_hbm.1, f32[16,64]{1,0:T(8,128)} %iw_hbm.1), custom_call_target="tpu_custom_call" | custom-call | tf_op jit(solution)/shard_map/index_grads/pallas_call | solution.py:453
  60.8 1.5 %finish.1 = (f32[16,4,128]{2,1,0:T(4,128)}, f32[128,128]{1,0:T(8,128)}) custom-call(f32[16,4,128]{2,1,0:T(4,128)} %get-tuple-element.4.query_ref, f32[128,128]{1,0:T(8,128)} %get-tuple-element.5.key_ref), custom_call_target="tpu_custom_call" | custom-call | tf_op jit(solution)/shard_map/finish/pallas_call | solution.py:506

commit v3 on v2

--- a/solution.py
+++ b/solution.py
@@ -45,7 +45,7 @@
     qraw, rx, qpack, qext, lse_all, lseb, kt, iqraw, qf, qjm, qt, iwv, wb, ik, ikt, wm, logits, mass, msend, mrecv,
     st_send, st_recv, terms, gk_send, gk_recv, gk_own, gq_send, gq_recv, gq_own,
     load_sem, q_ssem, q_rsem, l_ssem, l_rsem, m_ssem, m_rsem,
-    zl_send, zl_recv, zs_send, zs_recv, sib_send, sib_recv, st_ssem, st_rsem,
+    zl_send, zl_recv, zs_send, zs_recv, zb_send, zb_recv, sib_send, sib_recv, st_ssem, st_rsem,
     gk_ssem, gk_rsem, gq_ssem, gq_rsem,
 ):
     me_c = lax.axis_index("context")
@@ -174,7 +174,8 @@
         pair = jnp.concatenate([groups[g], groups[g + 4]], axis=1)
         qpack[0, 8, :, g * DIM : (g + 1) * DIM] = pair.astype(BF16)
 
-    cuts = (pl.ds(0, 4), pl.ds(4, 5))
+    cuts = (pl.ds(0, 3), pl.ds(3, 3), pl.ds(6, 3))
+    parts = len(cuts)
 
     def chain(i, part, long):
         source_slot = 0 if i == 1 else (slot_l(i - 1) if long else slot_r(i - 1))
@@ -185,27 +186,33 @@
             ssem.at[i - 1, part], rsem.at[i - 1, part], "context", next_c if long else prev_c,
         )
 
+    def last_hop(part):
+        return remote(
+            qpack.at[slot_l(3), cuts[part]], qpack.at[15, cuts[part]],
+            zb_send.at[part], zb_recv.at[part], "context", ctx_of(way, 1 - core),
+        )
+
     def to_sibling(slot):
-        target = {0: 1, 14: 15}.get(slot, slot + 2)
-        index = {0: 0, 14: 7}.get(slot, 1 + (slot - 2) // 4 * 2 + (slot - 2) % 4)
+        target = 1 if slot == 0 else slot + 2
+        index = 0 if slot == 0 else 1 + (slot - 2) // 4 * 2 + (slot - 2) % 4
         return remote(qpack.at[slot], qpack.at[target], sib_send.at[index], sib_recv.at[index], "context", sibling)
 
-    for part in range(2):
+    for part in range(parts):
         chain(1, part, True).start()
         chain(1, part, False).start()
     to_sibling(0).start()
 
-    def advance(i, part):
-        chain(i, part, True).wait_recv()
-        if i < 4:
+    def advance(i):
+        for part in range(parts):
+            chain(i, part, True).wait_recv()
             chain(i + 1, part, True).start()
+            if i == 3:
+                last_hop(part).start()
             chain(i, part, False).wait_recv()
             if i < 3:
                 chain(i + 1, part, False).start()
-        if part == 1:
-            to_sibling(slot_l(i)).start()
-            if i < 4:
-                to_sibling(slot_r(i)).start()
+        to_sibling(slot_l(i)).start()
+        to_sibling(slot_r(i)).start()
 
     def widen(first, count):
         for slot in range(first, first + count):
@@ -266,35 +273,29 @@
     loads[1].wait()
     arrived(lse_all, l_rsem)
     shifts()
-    advance(1, 0)
-    advance(1, 1)
+    for i in range(IDXH * ROWS // DIM):
+        at = pl.ds(i * DIM, DIM)
+        qt[:, at] = jnp.swapaxes(qjm[at, :].astype(F32), 0, 1).astype(BF16)
+    advance(1)
     loads[5].wait()
     to_sibling(0).wait_recv()
     widen(0, 2)
     piece(0, 2, 0, 4)
     deliver(0, 2)
-    advance(2, 0)
-    for i in range(IDXH * ROWS // DIM):
-        at = pl.ds(i * DIM, DIM)
-        qt[:, at] = jnp.swapaxes(qjm[at, :].astype(F32), 0, 1).astype(BF16)
-    advance(2, 1)
+    advance(2)
     siblings_of(1)
-    piece(slot_l(1), 4, 0, 3)
-    advance(3, 0)
-    piece(slot_l(1), 4, 3, 4)
+    piece(slot_l(1), 4, 0, 4)
     deliver(slot_l(1), 4)
-    advance(3, 1)
+    advance(3)
     siblings_of(2)
-    piece(slot_l(2), 4, 0, 3)
-    advance(4, 0)
-    piece(slot_l(2), 4, 3, 4)
+    piece(slot_l(2), 4, 0, 4)
     deliver(slot_l(2), 4)
     siblings_of(3)
-    piece(slot_l(3), 4, 0, 2)
-    advance(4, 1)
-    piece(slot_l(3), 4, 2, 4)
+    piece(slot_l(3), 4, 0, 4)
     deliver(slot_l(3), 4)
-    to_sibling(14).wait_recv()
+    for part in range(parts):
+        chain(4, part, True).wait_recv()
+        last_hop(part).wait_recv()
     widen(14, 2)
     piece(14, 2, 0, 4)
     deliver(14, 2)
@@ -354,17 +355,42 @@
 
     lax.fori_loop(0, KEYS // BIG, slope_tile, 0)
 
-    def gk_copy(owner):
-        return remote(gk_send.at[owner], gk_recv.at[me_h], gk_ssem.at[owner], gk_rsem.at[me_h], "heads", owner)
-
-    def key_tile(i, carry):
-        quad = lax.rem(me_h // 4 + 1 + i, 4)
-        at = pl.ds(pl.multiple_of(quad * BIG, BIG), BIG)
+    def term_tile(i, carry):
+        at = pl.ds(pl.multiple_of(i * BIG, BIG), BIG)
         slope = mass[:, at][None]
         for r in range(4):
             rows = pl.ds(r * TILE, TILE)
             term = wm[rows, at].reshape(TILE // ROWS, ROWS, BIG) * slope
             terms[rows, at] = term.reshape(TILE, BIG).astype(BF16)
+        return carry
+
+    lax.fori_loop(0, KEYS // BIG, term_tile, 0)
+
+    def gq_copy(owner):
+        return remote(gq_send.at[owner], gq_recv.at[me_c], gq_ssem.at[owner], gq_rsem.at[me_c], "context", owner)
+
+    def gk_copy(owner):
+        return remote(gk_send.at[owner], gk_recv.at[me_h], gk_ssem.at[owner], gk_rsem.at[me_h], "heads", owner)
+
+    def both_grads(i, carry):
+        chunk = lax.rem(me_c // 4 + 2 + (1 - 2 * lax.rem(i, 2)) * ((i + 1) // 2), 4)
+        rows = pl.ds(pl.multiple_of(chunk * TILE, TILE), TILE)
+        grad = jnp.dot(terms[rows, :], ik[...], preferred_element_type=F32)
+        for b in range(4):
+            owner = chunk * 4 + b
+            part = grad[b * 64 : (b + 1) * 64, :]
+            gq_send[owner] = part.astype(BF16)
+
+            @pl.when(owner != me_c)
+            def _():
+                gq_copy(owner).start()
+
+            @pl.when(owner == me_c)
+            def _():
+                gq_own[...] = part
+
+        quad = lax.rem(me_h // 4 + 2 + (1 - 2 * lax.rem(i, 2)) * ((i + 1) // 2), 4)
+        at = pl.ds(pl.multiple_of(quad * BIG, BIG), BIG)
         grad = jnp.dot(qt[...], terms[:, at], preferred_element_type=F32)
         for b in range(4):
             owner = quad * 4 + b
@@ -381,31 +407,25 @@
 
         return carry
 
-    lax.fori_loop(0, 4, key_tile, 0)
-
-    def gq_copy(owner):
-        return remote(gq_send.at[owner], gq_recv.at[me_c], gq_ssem.at[owner], gq_rsem.at[me_c], "context", owner)
-
-    def query_rows(i, carry):
-        chunk = lax.rem(me_c // 2 + 4 + (1 - 2 * lax.rem(i, 2)) * ((i + 1) // 2), 8)
-        rows = pl.ds(pl.multiple_of(chunk * DIM, DIM), DIM)
-        grad = jnp.dot(terms[rows, :], ik[...], preferred_element_type=F32)
-        for b in range(2):
-            owner = chunk * 2 + b
-            part = grad[b * 64 : (b + 1) * 64, :]
-            gq_send[owner] = part.astype(BF16)
-
-            @pl.when(owner != me_c)
-            def _():
-                gq_copy(owner).start()
-
-            @pl.when(owner == me_c)
-            def _():
-                gq_own[...] = part
-
-        return carry
-
-    lax.fori_loop(0, 8, query_rows, 0)
+    lax.fori_loop(0, 4, both_grads, 0)
+
+    for part in range(parts):
+        last_hop(part).wait_send()
+        for i in range(1, 5):
+            chain(i, part, True).wait_send()
+        for i in range(1, 4):
+            chain(i, part, False).wait_send()
+    for slot in (0, 2, 3, 6, 7, 10, 11):
+        to_sibling(slot).wait_send()
+    for slot in range(16):
+
+        @pl.when(source[slot] != me_h)
+        def _():
+            mass_copy(slot).wait_send()
+
+    for o in range(1, NC):
+        for copy in (q_copy, l_copy, stat_copy):
+            copy(o).wait_send()
 
     arrived(gk_recv, gk_rsem)
     key_sum = gk_own[...]
@@ -420,22 +440,7 @@
     for j in range(IDXH // NC):
         oq_ref[:, j, :] = query_sum[j * ROWS : (j + 1) * ROWS, :]
 
-    for part in range(2):
-        for i in range(1, 5):
-            chain(i, part, True).wait_send()
-        for i in range(1, 4):
-            chain(i, part, False).wait_send()
-    for slot in (0, 2, 3, 6, 7, 10, 11, 14):
-        to_sibling(slot).wait_send()
-    for slot in range(16):
-
-        @pl.when(source[slot] != me_h)
-        def _():
-            mass_copy(slot).wait_send()
-
     for o in range(1, NC):
-        for copy in (q_copy, l_copy, stat_copy):
-            copy(o).wait_send()
         gk_copy(plane(o)).wait_send()
         gq_copy(line(o)).wait_send()
 
@@ -490,10 +495,12 @@
             pltpu.VMEM((64, DIM), F32),
             dma((6,)),
             *[dma((16,))] * 6,
-            dma((4, 2)),
-            dma((4, 2)),
-            dma((3, 2)),
-            dma((3, 2)),
+            dma((4, 3)),
+            dma((4, 3)),
+            dma((3, 3)),
+            dma((3, 3)),
+            dma((3,)),
+            dma((3,)),
             dma((8,)),
             dma((8,)),
             *[dma((16,))] * 6,

time: 62.4 us -> 61.1 us (0.979)
  Pallas kernels: 61.6 us -> 60.3 us
    pallas_call x1, Pallas kernels: 60.1 us -> 58.8 us  [on_device(): pl.pallas_call(kernel, out_shape=(jax.ShapeDtypeStruct((ROWS, IDXH // NC,...]
where the time goes in v3:
time: 61.1 us; the launch traced here: 61 us
  Pallas kernels  60.3 us (99%)
  between operations  0.64 us (1%)
    pallas_call x1, Pallas kernels, on_device(): pl.pallas_call(kernel, out_shape=(jax.ShapeDtypeStruct((ROWS, IDXH // NC,...  58.8 us
    pallas_call x1, Pallas kernels, on_device(): pl.pallas_call(finish, out_shape=(jax.ShapeDtypeStruct((ROWS, IDXH // NC,...  1.5 us

profile of v3, /device:TPU:1, one launch (start us, length us, event | category | flops | bytes accessed | tf_op | source)
XLA Modules:
  0.0 61.0 jit_solution(10851197891860414270)
XLA Ops:
  0.6 58.8 %index_grads.1 = (f32[16,4,128]{2,1,0:T(4,128)}, f32[128,128]{1,0:T(8,128)}) custom-call(bf16[16,8,576]{2,1,0:T(8,128)(2,1)} %mq_hbm.1, bf16[576,2048]{1,0:T(8,128)(2,1)} %bitcast.2, f32[8,256]{1,0:T(8,128)} %bitcast.3, s32[256]{0:T(256)} %len_ref.1, bf16[16,64,128]{2,1,0:T(8,128)(2,1)} %iq_hbm.1, bf16[2048,128]{1,0:T(8,128)(2,1)} %ik_hbm.1, f32[16,64]{1,0:T(8,128)} %iw_hbm.1), custom_call_target="tpu_custom_call" | custom-call | tf_op jit(solution)/shard_map/index_grads/pallas_call | solution.py:458
  59.5 1.5 %finish.1 = (f32[16,4,128]{2,1,0:T(4,128)}, f32[128,128]{1,0:T(8,128)}) custom-call(f32[16,4,128]{2,1,0:T(4,128)} %get-tuple-element.4.query_ref, f32[128,128]{1,0:T(8,128)} %get-tuple-element.5.key_ref), custom_call_target="tpu_custom_call" | custom-call | tf_op jit(solution)/shard_map/finish/pallas_call | solution.py:513

commit v4 on v3

--- a/solution.py
+++ b/solution.py
@@ -119,9 +119,8 @@
     def l_copy(o):
         return remote(lse_hbm, lse_all.at[me_h], l_ssem.at[o], l_rsem.at[me_h], "heads", plane(o))
 
-    for copy in (q_copy, l_copy):
-        for o in range(1, NH):
-            copy(o).start()
+    for o in range(1, NH):
+        q_copy(o).start()
 
     def arrived(buffer, rsem):
         for o in range(1, NH):
@@ -164,16 +163,6 @@
         lax.fori_loop(0, KEYS // BIG, share_tile, jnp.zeros((ROWS, BIG), F32)), axis=1, keepdims=True
     )
 
-    arrived(rx, q_rsem)
-    groups = []
-    for g in range(8):
-        group = rx[2 * g : 2 * g + 2].astype(F32).reshape(ROWS, LAT)
-        qpack[0, g] = group[:, :WIDE].astype(BF16)
-        groups.append(group[:, WIDE:])
-    for g in range(4):
-        pair = jnp.concatenate([groups[g], groups[g + 4]], axis=1)
-        qpack[0, 8, :, g * DIM : (g + 1) * DIM] = pair.astype(BF16)
-
     cuts = (pl.ds(0, 3), pl.ds(3, 3), pl.ds(6, 3))
     parts = len(cuts)
 
@@ -197,10 +186,22 @@
         index = 0 if slot == 0 else 1 + (slot - 2) // 4 * 2 + (slot - 2) % 4
         return remote(qpack.at[slot], qpack.at[target], sib_send.at[index], sib_recv.at[index], "context", sibling)
 
+    arrived(rx, q_rsem)
+    groups = []
     for part in range(parts):
+        for g in range(3 * part, min(3 * part + 3, 8)):
+            group = rx[2 * g : 2 * g + 2].astype(F32).reshape(ROWS, LAT)
+            qpack[0, g] = group[:, :WIDE].astype(BF16)
+            groups.append(group[:, WIDE:])
+        if part == parts - 1:
+            for g in range(4):
+                pair = jnp.concatenate([groups[g], groups[g + 4]], axis=1)
+                qpack[0, 8, :, g * DIM : (g + 1) * DIM] = pair.astype(BF16)
         chain(1, part, True).start()
         chain(1, part, False).start()
     to_sibling(0).start()
+    for o in range(1, NH):
+        l_copy(o).start()
 
     def advance(i):
         for part in range(parts):
@@ -270,13 +271,13 @@
         to_sibling(slot_r(i)).wait_recv()
         widen(slot_l(i), 4)
 
-    loads[1].wait()
-    arrived(lse_all, l_rsem)
-    shifts()
     for i in range(IDXH * ROWS // DIM):
         at = pl.ds(i * DIM, DIM)
         qt[:, at] = jnp.swapaxes(qjm[at, :].astype(F32), 0, 1).astype(BF16)
     advance(1)
+    loads[1].wait()
+    arrived(lse_all, l_rsem)
+    shifts()
     loads[5].wait()
     to_sibling(0).wait_recv()
     widen(0, 2)
@@ -373,6 +374,22 @@
         return remote(gk_send.at[owner], gk_recv.at[me_h], gk_ssem.at[owner], gk_rsem.at[me_h], "heads", owner)
 
     def both_grads(i, carry):
+        quad = lax.rem(me_h // 4 + 2 + (1 - 2 * lax.rem(i, 2)) * ((i + 1) // 2), 4)
+        at = pl.ds(pl.multiple_of(quad * BIG, BIG), BIG)
+        grad = jnp.dot(qt[...], terms[:, at], preferred_element_type=F32)
+        for b in range(4):
+            owner = quad * 4 + b
+            part = grad[:, b * DIM : (b + 1) * DIM]
+            gk_send[owner] = part.astype(BF16)
+
+            @pl.when(owner != me_h)
+            def _():
+                gk_copy(owner).start()
+
+            @pl.when(owner == me_h)
+            def _():
+                gk_own[...] = part
+
         chunk = lax.rem(me_c // 4 + 2 + (1 - 2 * lax.rem(i, 2)) * ((i + 1) // 2), 4)
         rows = pl.ds(pl.multiple_of(chunk * TILE, TILE), TILE)
         grad = jnp.dot(terms[rows, :], ik[...], preferred_element_type=F32)
@@ -388,22 +405,6 @@
             @pl.when(owner == me_c)
             def _():
                 gq_own[...] = part
-
-        quad = lax.rem(me_h // 4 + 2 + (1 - 2 * lax.rem(i, 2)) * ((i + 1) // 2), 4)
-        at = pl.ds(pl.multiple_of(quad * BIG, BIG), BIG)
-        grad = jnp.dot(qt[...], terms[:, at], preferred_element_type=F32)
-        for b in range(4):
-            owner = quad * 4 + b
-            part = grad[:, b * DIM : (b + 1) * DIM]
-            gk_send[owner] = part.astype(BF16)
-
-            @pl.when(owner != me_h)
-            def _():
-                gk_copy(owner).start()
-
-            @pl.when(owner == me_h)
-            def _():
-                gk_own[...] = part
 
         return carry
 

time: 61.1 us -> 60.4 us (0.989)
  Pallas kernels: 60.3 us -> 59.6 us
    pallas_call x1, Pallas kernels: 58.8 us -> 58.1 us  [on_device(): pl.pallas_call(kernel, out_shape=(jax.ShapeDtypeStruct((ROWS, IDXH // NC,...]
where the time goes in v4:
time: 60.4 us; the launch traced here: 60.3 us
  Pallas kernels  59.6 us (99%)
  between operations  0.64 us (1%)
    pallas_call x1, Pallas kernels, on_device(): pl.pallas_call(kernel, out_shape=(jax.ShapeDtypeStruct((ROWS, IDXH // NC,...  58.1 us
    pallas_call x1, Pallas kernels, on_device(): pl.pallas_call(finish, out_shape=(jax.ShapeDtypeStruct((ROWS, IDXH // NC,...  1.5 us

profile of v4, /device:TPU:1, one launch (start us, length us, event | category | flops | bytes accessed | tf_op | source)
XLA Modules:
  0.0 60.3 jit_solution(1330690393818824564)
XLA Ops:
  0.6 58.1 %index_grads.1 = (f32[16,4,128]{2,1,0:T(4,128)}, f32[128,128]{1,0:T(8,128)}) custom-call(bf16[16,8,576]{2,1,0:T(8,128)(2,1)} %mq_hbm.1, bf16[576,2048]{1,0:T(8,128)(2,1)} %bitcast.2, f32[8,256]{1,0:T(8,128)} %bitcast.3, s32[256]{0:T(256)} %len_ref.1, bf16[16,64,128]{2,1,0:T(8,128)(2,1)} %iq_hbm.1, bf16[2048,128]{1,0:T(8,128)(2,1)} %ik_hbm.1, f32[16,64]{1,0:T(8,128)} %iw_hbm.1), custom_call_target="tpu_custom_call" | custom-call | tf_op jit(solution)/shard_map/index_grads/pallas_call | solution.py:459
  58.8 1.5 %finish.1 = (f32[16,4,128]{2,1,0:T(4,128)}, f32[128,128]{1,0:T(8,128)}) custom-call(f32[16,4,128]{2,1,0:T(4,128)} %get-tuple-element.4.query_ref, f32[128,128]{1,0:T(8,128)} %get-tuple-element.5.key_ref), custom_call_target="tpu_custom_call" | custom-call | tf_op jit(solution)/shard_map/finish/pallas_call | solution.py:514
